TPU v7x, 512 devices: a whole 4x8x8 slice. The times are simulated.
512 devices in a mesh: dom: 64 (over z_lo, y, core), col: 8 (over x, z_hi).
Axes of the slice: x: 4, y: 8, z: 8 (z_hi: 2, z_lo: 4; z = z_hi * 4 + z_lo), core: 2. Of those that a mesh axis runs over, the one named last changes fastest.
Arguments:
- features: bfloat16 [128, 16384], P('col', 'dom'), may hold values from -6 to 6
- cached_embed: bfloat16 [128, 16384], P('col'), may hold values from -6 to 6
- staleness: int32 [64], replicated, may hold values from 0 to 15, as said below
- node_counts: int32 [64], replicated, may hold values from 64 to 256, as said below
- neighbours: int32 [16, 16384], P(None, 'dom'), may hold values from 0 to 16383, as said below
- degrees: int32 [16384], P('dom'), may hold values from 1 to 16
- w_self: bfloat16 [128, 256], P('col'), may hold values from -0.5 to 0.5
- w_nbr: bfloat16 [128, 256], P('col'), may hold values from -0.5 to 0.5
- sage_bias: float32 [256], P('col'), may hold values from -3 to 3
- cotangent: bfloat16 [256, 16384], P('col', 'dom'), may hold values from -6 to 6
Outputs:
- activation: bfloat16 [256, 16384], P('col', 'dom')
- grad_feat: bfloat16 [128, 16384], P('col', 'dom')
- grad_self: float32 [128, 256], P('col')
- grad_nbr: float32 [128, 256], P('col')
- grad_bias: float32 [256], P('col')
Inputs may be any that keep to these rules, and one draw needn't show every extreme that they name: Exactly 16 partitions have staleness of 8 or more. `node_counts`: some partition has all 256 node slots live. `neighbours`: every neighbour slot names a live node slot; about half lie in the node's own partition.
All inputs are finite; a program needn't handle non-finite values.
Results may differ from a plain program's by a relative error of at most 0.015.
Values may be sent and summed in bfloat16 or wider, within the bound.
A program may use at most 64 MiB of HBM per device.

v0:
```python
import jax
import jax.numpy as jnp
from jax import lax
from jax.sharding import PartitionSpec as P

LIMIT = 8


def left_product(weight, data):
    return lax.dot_general(
        weight, data, (((0,), (0,)), ((), ())), preferred_element_type=jnp.float32
    )


def right_product(data, grads):
    return lax.dot_general(
        data, grads, (((1,), (1,)), ((), ())), preferred_element_type=jnp.float32
    )


def per_device(
    features,
    cached_embed,
    staleness,
    node_counts,
    neighbours,
    degrees,
    w_self,
    w_nbr,
    sage_bias,
    cotangent,
):
    col_width = features.shape[0]
    part_rows = features.shape[1]
    slot_count = neighbours.shape[0]
    my_index = lax.axis_index("dom")
    fresh_flag = (staleness >= LIMIT).astype(jnp.int32)
    my_fresh = fresh_flag[my_index]
    own_cache = lax.dynamic_slice_in_dim(cached_embed, my_index * part_rows, part_rows, 1)
    own_source = jnp.where(my_fresh == 1, features, own_cache)
    sources = lax.all_gather(own_source, "dom", axis=1, tiled=True)
    local_slot = jnp.arange(part_rows, dtype=jnp.int32)
    live_rows = (local_slot < node_counts[my_index]).astype(jnp.float32)
    slot_index = jnp.arange(slot_count, dtype=jnp.int32)
    used = (slot_index[:, None] < degrees[None, :]).astype(jnp.float32)
    weights = used * (live_rows / degrees.astype(jnp.float32))[None, :]
    gathered = sources[:, neighbours].astype(jnp.float32)
    aggregated = jnp.sum(weights[None, :, :] * gathered, axis=1).astype(jnp.bfloat16)
    partial_pre = left_product(w_self, features) + left_product(w_nbr, aggregated)
    pre_act = (
        lax.psum_scatter(
            partial_pre.astype(jnp.bfloat16), "col", scatter_dimension=0, tiled=True
        ).astype(jnp.float32)
        + sage_bias[:, None]
    )
    sigmoid = 1.0 / (1.0 + jnp.exp(-pre_act))
    activation = (live_rows[None, :] * pre_act * sigmoid).astype(jnp.bfloat16)
    grad_pre = (
        live_rows[None, :]
        * cotangent.astype(jnp.float32)
        * sigmoid
        * (1.0 + pre_act * (1.0 - sigmoid))
    ).astype(jnp.bfloat16)
    grad_full = lax.all_gather(grad_pre, "col", axis=0, tiled=True)
    self_part = right_product(features, grad_full)
    nbr_part = right_product(aggregated, grad_full)
    bias_part = jnp.sum(grad_pre.astype(jnp.float32), axis=1)
    grad_self, grad_nbr, grad_bias = lax.psum((self_part, nbr_part, bias_part), "dom")
    grad_agg = jnp.dot(w_nbr, grad_full, preferred_element_type=jnp.float32).astype(jnp.bfloat16)
    own_term = jnp.dot(w_self, grad_full, preferred_element_type=jnp.float32)
    spread = weights[None, :, :] * grad_agg.astype(jnp.float32)[:, None, :]
    total_rows = cached_embed.shape[1]
    contrib = (
        jnp.zeros((col_width, total_rows), jnp.float32)
        .at[:, neighbours.reshape(-1)]
        .add(spread.reshape(col_width, -1))
    )
    back = lax.psum_scatter(contrib, "dom", scatter_dimension=1, tiled=True)
    grad_feat = (own_term + my_fresh.astype(jnp.float32) * back).astype(jnp.bfloat16)
    return (activation, grad_feat, grad_self, grad_nbr, grad_bias)


def solution(mesh):
    placed = (
        P("col", "dom"),
        P("col", None),
        P(),
        P(),
        P(None, "dom"),
        P("dom"),
        P("col", None),
        P("col", None),
        P("col"),
        P("col", "dom"),
    )
    return jax.shard_map(
        per_device,
        mesh=mesh,
        in_specs=placed,
        out_specs=(P("col", "dom"), P("col", "dom"), P("col", None), P("col", None), P("col")),
        check_vma=False,
    )
```

profile of v0, /device:TPU:2, one launch (start us, length us, event | category | flops | bytes accessed | tf_op | source)
XLA Modules:
  0.0 577.7 jit_solution(13687929819668123944)
XLA Ops:
  7.2 0.0 copy-start
  7.2 0.0 reduce-scatter.3.cloned.1.call-start
  7.2 0.7 compare_convert_fusion
  7.9 1.2 dynamic_slice.9
  9.2 0.6 dynamic_slice.10
  9.8 0.7 fusion.12
  10.5 1.3 convert_divide_fusion
  11.8 0.7 fusion.14
  12.5 0.0 copy-done
  12.5 0.1 copy.21
  12.7 0.8 copy.16
  14.1 99.0 %all_gather.6 = bf16[16,16384]{0,1:T(8,128)(2,1)} all-gather(bf16[16,256]{0,1:T(8,128)(2,1)S(1)} %broadcast_select_fusion), channel_id=1, replica_groups=mesh['dom'=64,'col'=8] {'dom'}, dimensions={1}, use_global_device_ids=true | all-gather | bytes 532480 | tf_op jit(solution)/shard_map/all_gather | solution.py:41
  113.2 0.0 copy-start.4
  113.2 0.0 copy-start.1
  113.2 0.0 copy-start.3
  113.2 0.0 copy-start.2
  113.2 0.0 copy-start.5
  113.2 0.0 copy-start.6
  113.2 13.8 %gather_fusion = bf16[4096,16]{1,0:T(8,128)(2,1)S(1)} fusion(bf16[16,16384]{0,1:T(8,128)(2,1)} %all_gather.6, s32[4096]{0:T(1024)S(1)} %broadcast_clamp_fusion), kind=kCustom, calls=%fused_computation | custom fusion | bytes 278528 | tf_op jit(solution)/shard_map/gather | solution.py:47
  127.0 0.7 fusion.2
  127.7 0.0 copy-done.4
  127.7 0.2 convolution_bitcast_fusion
  128.0 0.0 copy-done.1
  128.0 0.0 copy-done.3
  128.0 0.9 fusion.4
  128.9 0.0 reduce-scatter.3.cloned.1.call-update
  128.9 0.0 reduce-scatter.5.cloned.1.call-start
  128.9 0.0 copy-done.2
  129.0 0.7 compare_convert_fusion.1
  129.7 84.0 %reduce-scatter.3.cloned.1.call-done = bf16[32,256]{1,0:T(8,128)(2,1)} async-done(((bf16[256,256]{1,0:T(8,128)(2,1)}), bf16[32,256]{1,0:T(8,128)(2,1)}) %reduce-scatter.3.cloned.1.call-update) | async-done | bytes 16400 | tf_op jit(solution)/shard_map/reduce_scatter | solution.py:51
  213.6 0.0 copy-done.5
  213.6 0.0 copy-done.6
  213.6 1.5 convert_reduce_fusion
  215.2 42.2 %all_gather.7 = bf16[256,256]{1,0:T(8,128)(2,1)S(1)} all-gather(bf16[32,256]{1,0:T(8,128)(2,1)S(1)} %get-tuple-element.9), channel_id=1, replica_groups=mesh['dom'=64,'col'=8] {'col'}, dimensions={0}, use_global_device_ids=true | all-gather | bytes 147456 | tf_op jit(solution)/shard_map/all_gather | solution.py:64
  257.3 0.1 fusion.8
  257.5 0.1 copy.18
  257.6 0.6 bitcast_multiply_fusion
  258.2 26.1 %scatter_custom_fusion = f32[16,16384]{0,1:T(8,128)} fusion(s32[4096]{0:T(1024)S(1)} %bitcast.50, f32[]{:T(128)} %constant.14.clone.1, f32[16,4096]{0,1:T(8,128)S(1)} %bitcast_multiply_fusion), kind=kCustom, calls=%fused_computation.2 | custom fusion | flops 65536 | bytes 3145732 | tf_op jit(solution)/shard_map/scatter-add | solution.py:76
  284.3 6.0 %copy.19 = f32[16,16384]{1,0:T(8,128)} copy(f32[16,16384]{0,1:T(8,128)} %scatter_custom_fusion) | data formatting | bytes 2097152 | tf_op jit(solution)/shard_map/scatter-add | solution.py:76
  290.3 0.0 reduce-scatter.5.cloned.1.call-update
  291.0 0.1 convolution_bitcast_fusion.2
  291.1 0.2 fusion.15
  291.3 265.0 %all-reduce = (f32[16,256]{1,0:T(8,128)}, f32[16,256]{1,0:T(8,128)}, f32[32]{0:T(128)}) all-reduce(f32[16,256]{1,0:T(8,128)S(1)} %convolution_bitcast_fusion.2, f32[16,256]{1,0:T(8,128)S(1)} %fusion.15, f32[32]{0:T(128)S(1)} %get-tuple-element.8), channel_id=1, replica_groups=mesh['dom'=64,'col'=8] {'dom'}, use_global_device_ids=true, to_apply=%region_4.5 | all-reduce | flops 8224 | bytes 65792 | tf_op jit(solution)/shard_map/psum | solution.py:68
  556.3 13.1 %reduce-scatter.5.cloned.1.call-done = f32[16,256]{1,0:T(8,128)} async-done(((f32[16,16384]{1,0:T(8,128)}), f32[16,256]{1,0:T(8,128)}) %reduce-scatter.5.cloned.1.call-update) | async-done | bytes 16400 | tf_op jit(solution)/shard_map/reduce_scatter | solution.py:78
  569.4 1.5 fusion.6
  (7 shorter events, 0.1 us)
Async XLA Ops:
  7.2 5.4 copy-start
  7.2 206.4 %reduce-scatter.3.cloned.1.call-start = ((), (), s32[]{:S(2)}) async-start(), calls=%async_computation.2 | async-start | bytes 147456 | tf_op jit(solution)/shard_map/reduce_scatter | solution.py:51
  113.2 14.6 %copy-start.4 = (bf16[16,256]{1,0:T(8,128)(2,1)S(1)}, bf16[16,256]{1,0:T(8,128)(2,1)}, u32[]{:S(2)}) copy-start(bf16[16,256]{1,0:T(8,128)(2,1)} %param.17) | copy-start | bytes 24580
  113.2 14.8 %copy-start.1 = (bf16[16,256]{1,0:T(8,128)(2,1)S(1)}, bf16[16,256]{1,0:T(8,128)(2,1)}, u32[]{:S(2)}) copy-start(bf16[16,256]{1,0:T(8,128)(2,1)} %param.10) | copy-start | bytes 24580
  113.2 14.8 %copy-start.3 = (bf16[16,256]{1,0:T(8,128)(2,1)S(1)}, bf16[16,256]{1,0:T(8,128)(2,1)}, u32[]{:S(2)}) copy-start(bf16[16,256]{1,0:T(8,128)(2,1)} %param.16) | copy-start | bytes 24580
  113.2 15.8 %copy-start.2 = (s32[16,256]{1,0:T(8,128)S(1)}, s32[16,256]{1,0:T(8,128)}, u32[]{:S(2)}) copy-start(s32[16,256]{1,0:T(8,128)} %param.14) | copy-start | bytes 49156
  113.2 100.5 %copy-start.5 = (bf16[32,256]{1,0:T(8,128)(2,1)S(1)}, bf16[32,256]{1,0:T(8,128)(2,1)}, u32[]{:S(2)}) copy-start(bf16[32,256]{1,0:T(8,128)(2,1)} %param.19) | copy-start | bytes 49156
  113.2 100.5 %copy-start.6 = (f32[32]{0:T(128)S(1)}, f32[32]{0:T(128)}, u32[]{:S(2)}) copy-start(f32[32]{0:T(128)} %param.18) | copy-start | bytes 388
  128.9 440.5 %reduce-scatter.5.cloned.1.call-start = ((), (), s32[]{:S(2)}) async-start(), calls=%async_computation.3 | async-start | bytes 1064960 | tf_op jit(solution)/shard_map/reduce_scatter | solution.py:78
Sparse Core Ops, SparseCore 0:
  129.0 84.5 reduce-scatter.2
  290.4 278.9 reduce-scatter.4
where the time goes:
time: 578 us
  blocking collectives  406 us (70%)
  waiting for transfers between devices  97.1 us (17%)
  other arithmetic  33.1 us (6%)
  local copies, waits for them, and re-layouts  22.8 us (4%)
  between operations  15.5 us (3%)
    psum x1, blocking collectives, per_device(): lax.psum((self_part, nbr_part, bias_part), 'dom')  265 us
    all_gather x1, blocking collectives, per_device(): sources = lax.all_gather(own_source, 'dom', axis=1, tiled=True)  99 us
    reduce_scatter x1, waiting for transfers between devices, per_device(): lax.psum_scatter(partial_pre.astype(jnp.bfloat16), 'col', scatter_dimensi...  84 us
    all_gather x1, blocking collectives, per_device(): grad_full = lax.all_gather(grad_pre, 'col', axis=0, tiled=True)  42.2 us
    scatter-add x1, other arithmetic, per_device(): contrib = jnp.zeros((col_width, total_rows), jnp.float32).at[:, neighbour...  26.1 us
    gather x1, local copies, waits for them, and re-layouts, per_device(): gathered = sources[:, neighbours].astype(jnp.float32)  13.8 us
    reduce_scatter x1, waiting for transfers between devices, per_device(): back = lax.psum_scatter(contrib, 'dom', scatter_dimension=1, tiled=True)  13.1 us
  transfers between devices with their start and end apart: 2, of which 2 were waited for; matrix products, arithmetic and copies ran while one was open for 0% of the time, Pallas kernels for 0%

commit v1 on v0

--- a/solution.py
+++ b/solution.py
@@ -38,7 +38,9 @@
     my_fresh = fresh_flag[my_index]
     own_cache = lax.dynamic_slice_in_dim(cached_embed, my_index * part_rows, part_rows, 1)
     own_source = jnp.where(my_fresh == 1, features, own_cache)
-    sources = lax.all_gather(own_source, "dom", axis=1, tiled=True)
+    sources = jnp.concatenate(
+        lax.all_to_all(jnp.stack([own_source] * lax.axis_size("dom")), "dom", 0, 0), axis=1
+    )
     local_slot = jnp.arange(part_rows, dtype=jnp.int32)
     live_rows = (local_slot < node_counts[my_index]).astype(jnp.float32)
     slot_index = jnp.arange(slot_count, dtype=jnp.int32)

time: 578 us -> 513 us (0.89)
  the two profiles are of different devices: /device:TPU:2 before, /device:TPU:4 now
where the time goes in v1:
time: 513 us; the launch traced here: 512 us
  blocking collectives  307 us (60%)
  waiting for transfers between devices  113 us (22%)
  other arithmetic  33.7 us (7%)
  local copies, waits for them, and re-layouts  26.4 us (5%)
  between operations  15.5 us (3%)
  starting transfers between devices  13.6 us (3%)
    psum x1, blocking collectives, per_device(): lax.psum((self_part, nbr_part, bias_part), 'dom')  265 us
    reduce_scatter x1, waiting for transfers between devices, per_device(): lax.psum_scatter(partial_pre.astype(jnp.bfloat16), 'col', scatter_dimensi...  85.2 us
    all_gather x1, blocking collectives, per_device(): grad_full = lax.all_gather(grad_pre, 'col', axis=0, tiled=True)  41.9 us
    scatter-add x1, other arithmetic, per_device(): contrib = jnp.zeros((col_width, total_rows), jnp.float32).at[:, neighbour...  26.1 us
    reduce_scatter x1, waiting for transfers between devices, per_device(): back = lax.psum_scatter(contrib, 'dom', scatter_dimension=1, tiled=True)  14.5 us
    gather x1, local copies, waits for them, and re-layouts, per_device(): gathered = sources[:, neighbours].astype(jnp.float32)  13.8 us
    all_to_all x1, starting transfers between devices, per_device(): lax.all_to_all(jnp.stack([own_source] * lax.axis_size('dom')), 'dom', 0, 0)  13.5 us
    all_to_all x1, waiting for transfers between devices, per_device(): lax.all_to_all(jnp.stack([own_source] * lax.axis_size('dom')), 'dom', 0, 0)  13 us
  transfers between devices with their start and end apart: 3, of which 3 were waited for; matrix products, arithmetic and copies ran while one was open for 1% of the time, Pallas kernels for 0%

profile of v1, /device:TPU:4, one launch (start us, length us, event | category | flops | bytes accessed | tf_op | source)
XLA Modules:
  0.0 512.0 jit_solution(12307607096361422659)
XLA Ops:
  7.2 0.0 copy-start
  7.2 0.7 compare_convert_fusion
  7.8 0.6 dynamic_slice.10
  9.1 0.7 dynamic-slice_select_fusion
  9.8 0.8 stack.2
  10.6 13.5 %all-to-all-start = ((bf16[64,16,256]{2,1,0:T(8,128)(2,1)}), bf16[64,16,256]{2,1,0:T(8,128)(2,1)S(1)}, u32[]{:S(2)}, u32[]{:S(2)}) async-start(bf16[64,16,256]{2,1,0:T(8,128)(2,1)} %stack.2), calls=%async_computation | async-start | bytes 1048576 | tf_op jit(solution)/shard_map/all_to_all | solution.py:42
  24.2 0.0 reduce-scatter.3.cloned.1.call-start
  24.2 1.2 dynamic_slice.9
  25.5 0.7 copy.25
  26.2 0.7 fusion.12
  26.9 1.3 convert_divide_fusion
  28.3 0.7 fusion.14
  29.0 13.0 %all-to-all-done = bf16[64,16,256]{2,1,0:T(8,128)(2,1)S(1)} async-done(((bf16[64,16,256]{2,1,0:T(8,128)(2,1)}), bf16[64,16,256]{2,1,0:T(8,128)(2,1)S(1)}, u32[]{:S(2)}, u32[]{:S(2)}) %all-to-all-start) | async-done | bytes 524320 | tf_op jit(solution)/shard_map/all_to_all | solution.py:42
  42.0 3.1 copy.19
  45.1 0.0 copy-start.1
  45.1 0.0 copy-start.2
  45.1 0.0 copy-start.3
  45.1 0.0 copy-start.4
  45.1 13.8 %gather_fusion = bf16[4096,16]{1,0:T(8,128)(2,1)S(1)} fusion(bf16[16,16384]{0,1:T(8,128)(2,1)} %bitcast.47, s32[4096]{0:T(1024)S(1)} %broadcast_clamp_fusion), kind=kCustom, calls=%fused_computation | custom fusion | bytes 278528 | tf_op jit(solution)/shard_map/gather | solution.py:49
  58.9 0.7 fusion.2
  59.6 0.0 copy-done
  59.6 0.2 convolution_bitcast_fusion
  59.8 0.0 copy-done.1
  59.9 0.0 copy-done.2
  59.9 0.9 fusion.4
  60.7 0.0 reduce-scatter.3.cloned.1.call-update
  60.8 0.0 reduce-scatter.5.cloned.1.call-start
  60.9 0.7 compare_convert_fusion.1
  61.5 85.2 %reduce-scatter.3.cloned.1.call-done = bf16[32,256]{1,0:T(8,128)(2,1)} async-done(((bf16[256,256]{1,0:T(8,128)(2,1)}), bf16[32,256]{1,0:T(8,128)(2,1)}) %reduce-scatter.3.cloned.1.call-update) | async-done | bytes 16400 | tf_op jit(solution)/shard_map/reduce_scatter | solution.py:53
  146.7 0.0 copy-done.3
  146.7 0.0 copy-done.4
  146.7 1.5 convert_reduce_fusion
  148.3 41.9 %all_gather.3 = bf16[256,256]{1,0:T(8,128)(2,1)S(1)} all-gather(bf16[32,256]{1,0:T(8,128)(2,1)S(1)} %get-tuple-element.9), channel_id=1, replica_groups=mesh['dom'=64,'col'=8] {'col'}, dimensions={0}, use_global_device_ids=true | all-gather | bytes 147456 | tf_op jit(solution)/shard_map/all_gather | solution.py:66
  190.2 0.1 fusion.8
  190.3 0.1 copy.21
  190.4 0.6 bitcast_multiply_fusion
  191.1 26.1 %scatter_custom_fusion = f32[16,16384]{0,1:T(8,128)} fusion(s32[4096]{0:T(1024)S(1)} %bitcast.54, f32[]{:T(128)} %constant.14.clone.1, f32[16,4096]{0,1:T(8,128)S(1)} %bitcast_multiply_fusion), kind=kCustom, calls=%fused_computation.2 | custom fusion | flops 65536 | bytes 3145732 | tf_op jit(solution)/shard_map/scatter-add | solution.py:78
  217.2 6.0 %copy.22 = f32[16,16384]{1,0:T(8,128)} copy(f32[16,16384]{0,1:T(8,128)} %scatter_custom_fusion) | data formatting | bytes 2097152 | tf_op jit(solution)/shard_map/scatter-add | solution.py:78
  223.2 0.0 reduce-scatter.5.cloned.1.call-update
  223.8 0.1 convolution_bitcast_fusion.2
  224.0 0.2 fusion.15
  224.2 265.0 %all-reduce = (f32[16,256]{1,0:T(8,128)}, f32[16,256]{1,0:T(8,128)}, f32[32]{0:T(128)}) all-reduce(f32[16,256]{1,0:T(8,128)S(1)} %convolution_bitcast_fusion.2, f32[16,256]{1,0:T(8,128)S(1)} %fusion.15, f32[32]{0:T(128)S(1)} %get-tuple-element.8), channel_id=1, replica_groups=mesh['dom'=64,'col'=8] {'dom'}, use_global_device_ids=true, to_apply=%region_4.5 | all-reduce | flops 8224 | bytes 65792 | tf_op jit(solution)/shard_map/psum | solution.py:70
  489.1 14.5 %reduce-scatter.5.cloned.1.call-done = f32[16,256]{1,0:T(8,128)} async-done(((f32[16,16384]{1,0:T(8,128)}), f32[16,256]{1,0:T(8,128)}) %reduce-scatter.5.cloned.1.call-update) | async-done | bytes 16400 | tf_op jit(solution)/shard_map/reduce_scatter | solution.py:80
  503.7 1.5 fusion.6
  (4 shorter events, 0.0 us)
Async XLA Ops:
  7.2 52.4 %copy-start = (bf16[16,256]{1,0:T(8,128)(2,1)S(1)}, bf16[16,256]{1,0:T(8,128)(2,1)}, u32[]{:S(2)}) copy-start(bf16[16,256]{1,0:T(8,128)(2,1)} %param.17) | copy-start | bytes 24580
  10.6 31.3 %all-to-all-start = ((bf16[64,16,256]{2,1,0:T(8,128)(2,1)}), bf16[64,16,256]{2,1,0:T(8,128)(2,1)S(1)}, u32[]{:S(2)}, u32[]{:S(2)}) async-start(bf16[64,16,256]{2,1,0:T(8,128)(2,1)} %stack.2), calls=%async_computation | async-start | bytes 1048576 | tf_op jit(solution)/shard_map/all_to_all | solution.py:42
  24.2 122.5 %reduce-scatter.3.cloned.1.call-start = ((), (), s32[]{:S(2)}) async-start(), calls=%async_computation.3 | async-start | bytes 147456 | tf_op jit(solution)/shard_map/reduce_scatter | solution.py:53
  45.1 14.8 %copy-start.1 = (bf16[16,256]{1,0:T(8,128)(2,1)S(1)}, bf16[16,256]{1,0:T(8,128)(2,1)}, u32[]{:S(2)}) copy-start(bf16[16,256]{1,0:T(8,128)(2,1)} %param.10) | copy-start | bytes 24580
  45.1 14.8 %copy-start.2 = (bf16[16,256]{1,0:T(8,128)(2,1)S(1)}, bf16[16,256]{1,0:T(8,128)(2,1)}, u32[]{:S(2)}) copy-start(bf16[16,256]{1,0:T(8,128)(2,1)} %param.16) | copy-start | bytes 24580
  45.1 101.7 %copy-start.3 = (bf16[32,256]{1,0:T(8,128)(2,1)S(1)}, bf16[32,256]{1,0:T(8,128)(2,1)}, u32[]{:S(2)}) copy-start(bf16[32,256]{1,0:T(8,128)(2,1)} %param.19) | copy-start | bytes 49156
  45.1 101.7 %copy-start.4 = (f32[32]{0:T(128)S(1)}, f32[32]{0:T(128)}, u32[]{:S(2)}) copy-start(f32[32]{0:T(128)} %param.18) | copy-start | bytes 388
  60.8 442.9 %reduce-scatter.5.cloned.1.call-start = ((), (), s32[]{:S(2)}) async-start(), calls=%async_computation.4 | async-start | bytes 1064960 | tf_op jit(solution)/shard_map/reduce_scatter | solution.py:80
Sparse Core Ops, SparseCore 0:
  60.9 85.8 reduce-scatter.2
  223.3 280.3 reduce-scatter.4
